TPU v7x, 32 devices: a whole 2x2x4 slice. The times are simulated.
32 devices in a mesh: slab: 8 (over z, x), head: 4 (over y, core).
Axes of the slice: x: 2, y: 2, z: 4, core: 2. Of those that a mesh axis runs over, the one named last changes fastest.
Arguments:
- atom_feats: bfloat16 [2, 4096, 128], P(None, 'slab'), may hold values from -16 to 16
- pair_feats: bfloat16 [4096, 16, 128], P('slab'), may hold values from -8 to 330
- tok_slot: int32 [4096], P('slab'), may hold values from 0 to 255, as said below
- w_proj: bfloat16 [4, 128, 128], P(None, None, 'head'), may hold values from -0.5 to 0.5
- w_out: bfloat16 [128, 128], P('head'), may hold values from -0.5 to 0.5
- w_pair: bfloat16 [16, 4], P(None, 'head'), may hold values from -1.2 to 1.2
- w_tok: bfloat16 [128, 768], P(None, 'head'), may hold values from -0.5 to 0.5
- d_tok: bfloat16 [2, 256, 768], P(None, 'slab', 'head'), may hold values from -6 to 6
Outputs:
- tok_act: bfloat16 [2, 256, 768], P(None, 'slab', 'head')
- grad_proj: float32 [4, 128, 128], P(None, None, 'head')
- grad_out: float32 [128, 128], P('head')
- grad_pair: float32 [16, 4], P(None, 'head')
- grad_tok: float32 [128, 768], P(None, 'head')
Inputs may be any that keep to these rules, and one draw needn't show every extreme that they name: `tok_slot`: never falling. The atoms s * 512 to (s + 1) * 512 - 1 use slots s * 32 to s * 32 + n - 1, each at least once, with n from 16 to 32; the first of these atoms is in slot s * 32. The last slab and one other use all 32 slots.
All inputs are finite; a program needn't handle non-finite values.
Results may differ from a plain program's by a relative error of at most 0.023.
Values may be sent and summed in bfloat16 or wider, within the bound.
A program may use at most 64 MiB of HBM per device.

v0:
```python
import jax
import jax.numpy as jnp
from jax import lax
from jax.sharding import PartitionSpec as P

Q_WIN = 32
K_WIN = 128
RIM = 48
EPSILON = 1e-05


def extended_2(cells, sides, width):
    for axis, dim in sides:
        count = lax.axis_size(axis)
        ends = count - 1
        head = lax.slice_in_dim(cells, 0, width, axis=dim)
        tail = lax.slice_in_dim(cells, cells.shape[dim] - width, cells.shape[dim], axis=dim)
        cells = jnp.concatenate(
            [
                lax.ppermute(tail, axis, [(i, (i + 1) % count) for i in range(ends)]),
                cells,
                lax.ppermute(head, axis, [((i + 1) % count, i) for i in range(ends)]),
            ],
            axis=dim,
        )
    return cells


def key_windows(extended, block_count):
    leading = extended.shape[:-2]
    last_width = extended.shape[-1]
    row_total = block_count * Q_WIN
    pieces = []
    for offset in range(K_WIN // Q_WIN):
        segment = lax.slice_in_dim(
            extended, Q_WIN * offset, Q_WIN * offset + row_total, axis=extended.ndim - 2
        )
        pieces.append(segment.reshape(leading + (block_count, Q_WIN, last_width)))
    return jnp.concatenate(pieces, axis=-2)


def key_unwindowed_rows(windowed, block_count):
    leading = windowed.shape[:-3]
    last_width = windowed.shape[-1]
    row_total = block_count * Q_WIN
    margin = K_WIN - Q_WIN
    summed = None
    for offset in range(K_WIN // Q_WIN):
        segment = windowed[..., Q_WIN * offset : Q_WIN * (offset + 1), :].reshape(
            leading + (row_total, last_width)
        )
        padding = [(0, 0)] * len(leading) + [(Q_WIN * offset, margin - Q_WIN * offset), (0, 0)]
        segment = jnp.pad(segment, padding)
        summed = segment if summed is None else summed + segment
    return summed


def on_device(atom_feats, pair_feats, tok_slot, w_proj, w_out, w_pair, w_tok, d_tok):
    samples, atom_count, feature_width = atom_feats.shape
    head_width = w_proj.shape[2]
    block_count = atom_count // Q_WIN
    slot_count = d_tok.shape[1]
    slab_index = lax.axis_index("slab")
    slab_total = lax.axis_size("slab")
    score_scale = head_width ** (-0.5)
    feats_float = atom_feats.astype(jnp.float32)
    centered = feats_float - jnp.mean(feats_float, axis=2, keepdims=True)
    variance = jnp.mean(centered * centered, axis=2, keepdims=True)
    normed = (centered * lax.rsqrt(variance + EPSILON)).astype(jnp.bfloat16)
    projected = jnp.einsum("saw,fwd->fsad", normed, w_proj, preferred_element_type=jnp.float32)
    queries = (projected[0] * score_scale).astype(jnp.bfloat16)
    keys_local = projected[1].astype(jnp.bfloat16)
    values_local = projected[2].astype(jnp.bfloat16)
    gating = jax.nn.sigmoid(projected[3])
    stacked = jnp.stack([keys_local, values_local])
    extended = extended_2(stacked, (("slab", 2),), RIM)
    windowed = key_windows(extended, block_count)
    key_window_rows = windowed[0]
    value_window_rows = windowed[1]
    query_block_rows = queries.reshape(samples, block_count, Q_WIN, head_width)
    pair_bias_terms = jnp.einsum(
        "acj,c->aj", pair_feats, w_pair[:, 0], preferred_element_type=jnp.float32
    )
    pair_bias_terms = pair_bias_terms.reshape(block_count, Q_WIN, K_WIN)
    positions = (
        slab_index * atom_count
        + Q_WIN * jnp.arange(block_count, dtype=jnp.int32)[:, None]
        - RIM
        + jnp.arange(K_WIN, dtype=jnp.int32)[None, :]
    )
    in_range = (positions >= 0) & (positions < atom_count * slab_total)
    attention_scores = (
        jnp.einsum(
            "sbqd,sbkd->sbqk", query_block_rows, key_window_rows, preferred_element_type=jnp.float32
        )
        + pair_bias_terms[None]
    )
    attention_scores = jnp.where(in_range[None, :, None, :], attention_scores, -jnp.inf)
    highest = jnp.max(attention_scores, axis=3, keepdims=True)
    exponent = jnp.exp(attention_scores - highest)
    attn_weights = exponent / jnp.sum(exponent, axis=3, keepdims=True)
    weight_half_precision = attn_weights.astype(jnp.bfloat16)
    attended_output = jnp.einsum(
        "sbqk,sbkd->sbqd",
        weight_half_precision,
        value_window_rows,
        preferred_element_type=jnp.float32,
    )
    attended_output = attended_output.reshape(samples, atom_count, head_width)
    heads_out = (gating * attended_output).astype(jnp.bfloat16)
    head_part = jnp.einsum(
        "nsad,ndw->nsaw",
        lax.all_gather(heads_out[None], "head", axis=0, tiled=True),
        lax.all_gather(w_out[None], "head", axis=0, tiled=True),
        preferred_element_type=jnp.float32,
    )
    rounded = lax.optimization_barrier(head_part.astype(jnp.bfloat16)).astype(jnp.float32)
    attn_sum = jnp.sum(rounded, axis=0)
    mixed_half = (feats_float + attn_sum).astype(jnp.bfloat16)
    pre_act = jnp.einsum("saw,wh->sah", mixed_half, w_tok, preferred_element_type=jnp.float32)
    act_gate = jax.nn.sigmoid(pre_act)
    atom_act = (pre_act * act_gate).astype(jnp.bfloat16)
    own_slots = slab_index * slot_count + jnp.arange(slot_count, dtype=jnp.int32)
    member = (tok_slot[:, None] == own_slots[None, :]).astype(jnp.bfloat16)
    counts = jnp.sum(member, axis=0, dtype=jnp.float32)
    divisor = jnp.maximum(counts, 1.0)
    token_sums = jnp.einsum("at,sah->sth", member, atom_act, preferred_element_type=jnp.float32)
    tok_act = (token_sums / divisor[None, :, None]).astype(jnp.bfloat16)
    tok_grad = (d_tok.astype(jnp.float32) / divisor[None, :, None]).astype(jnp.bfloat16)
    spread = jnp.einsum("at,sth->sah", member, tok_grad, preferred_element_type=jnp.float32)
    slope = act_gate * (1.0 + pre_act * (1.0 - act_gate))
    act_grad = (spread * slope).astype(jnp.bfloat16)
    grad_tok_local = jnp.einsum(
        "saw,sah->wh", mixed_half, act_grad, preferred_element_type=jnp.float32
    )
    mixed_terms = jnp.einsum("sah,wh->saw", act_grad, w_tok, preferred_element_type=jnp.float32)
    mixed_grad = lax.psum(mixed_terms.astype(jnp.bfloat16), "head")
    out_grad = jnp.einsum("saw,dw->sad", mixed_grad, w_out, preferred_element_type=jnp.float32)
    grad_out_local = jnp.einsum(
        "sad,saw->dw", heads_out, mixed_grad, preferred_element_type=jnp.float32
    )
    att_grad = (gating * out_grad).astype(jnp.bfloat16)
    gate_grad = (out_grad * attended_output * gating * (1.0 - gating)).astype(jnp.bfloat16)
    attention_block_rows = att_grad.reshape(samples, block_count, Q_WIN, head_width)
    probability_gradient = jnp.einsum(
        "sbqd,sbkd->sbqk",
        attention_block_rows,
        value_window_rows,
        preferred_element_type=jnp.float32,
    )
    score_grad = (
        attn_weights
        * (
            probability_gradient
            - jnp.sum(attn_weights * probability_gradient, axis=3, keepdims=True)
        )
    ).astype(jnp.bfloat16)
    query_gradient = score_scale * jnp.einsum(
        "sbqk,sbkd->sbqd", score_grad, key_window_rows, preferred_element_type=jnp.float32
    )
    query_gradient = query_gradient.reshape(samples, atom_count, head_width).astype(jnp.bfloat16)
    key_win_grad = jnp.einsum(
        "sbqk,sbqd->sbkd", score_grad, query_block_rows, preferred_element_type=jnp.float32
    )
    value_win_grad = jnp.einsum(
        "sbqk,sbqd->sbkd",
        weight_half_precision,
        attention_block_rows,
        preferred_element_type=jnp.float32,
    )
    spilled = key_unwindowed_rows(jnp.stack([key_win_grad, value_win_grad]), block_count)
    rim_local = jnp.concatenate([spilled[:, :, :RIM], spilled[:, :, RIM + atom_count :]], axis=2)
    returned = extended_2(rim_local.astype(jnp.bfloat16), (("slab", 2),), RIM).astype(
        rim_local.dtype
    )
    from_before = returned[:, :, :RIM]
    from_after = returned[:, :, 3 * RIM :]
    own_part = spilled[:, :, RIM : RIM + atom_count]
    own_part = own_part + jnp.pad(from_before, ((0, 0), (0, 0), (0, atom_count - RIM), (0, 0)))
    own_part = own_part + jnp.pad(from_after, ((0, 0), (0, 0), (atom_count - RIM, 0), (0, 0)))
    kv_grad = own_part.astype(jnp.bfloat16)
    grads_stack = jnp.stack([query_gradient, kv_grad[0], kv_grad[1], gate_grad])
    grad_proj_local = jnp.einsum(
        "saw,fsad->fwd", normed, grads_stack, preferred_element_type=jnp.float32
    )
    bias_grad = (
        jnp.sum(score_grad, axis=0, dtype=jnp.float32)
        .astype(jnp.bfloat16)
        .reshape(atom_count, K_WIN)
    )
    grad_pair_local = jnp.einsum(
        "acj,aj->c", pair_feats, bias_grad, preferred_element_type=jnp.float32
    )[:, None]
    factor = (samples * atom_count * slab_total) ** (-0.5)
    grad_proj_total, grad_out_total, grad_pair_total, grad_tok_total = lax.psum(
        (grad_proj_local, grad_out_local, grad_pair_local, grad_tok_local), "slab"
    )
    return (
        tok_act,
        grad_proj_total * factor,
        grad_out_total * factor,
        grad_pair_total * factor,
        grad_tok_total * factor,
    )


def solution(mesh):
    return jax.shard_map(
        on_device,
        mesh=mesh,
        in_specs=(
            P(None, "slab", None),
            P("slab", None, None),
            P("slab"),
            P(None, None, "head"),
            P("head", None),
            P(None, "head"),
            P(None, "head"),
            P(None, "slab", "head"),
        ),
        out_specs=(
            P(None, "slab", "head"),
            P(None, None, "head"),
            P("head", None),
            P(None, "head"),
            P(None, "head"),
        ),
        check_vma=False,
    )
```

profile of v0, /device:TPU:0, one launch (start us, length us, event | category | flops | bytes accessed | tf_op | source)
XLA Modules:
  0.0 244.7 jit_solution(9373553838993672769)
XLA Ops:
  7.2 1.2 convert_reduce_fusion.1
  8.5 1.3 fusion.14
  9.9 1.5 fusion.76
  11.4 4.9 %collective-permute-start = (bf16[2,2,48,32]{2,3,0,1:T(8,128)(2,1)S(1)}, bf16[2,2,48,32]{2,3,0,1:T(8,128)(2,1)S(1)}, u32[]{:S(2)}, u32[]{:S(2)}) collective-permute-start(bf16[2,2,48,32]{2,3,0,1:T(8,128)(2,1)S(1)} %get-tuple-element.19), channel_id=1, source_target_pairs={{0,4},{4,8},{8,12},{12,16},{16,20},{20,24},{24,28},{1,5},{5,9},{9,... | collective-permute-start | bytes 36872 | tf_op jit(solution)/shard_map/ppermute | solution.py:20
  16.3 1.3 collective-permute-start.1
  17.6 0.7 slice.103
  18.3 0.9 convert_reduce_fusion.2
  19.2 0.5 broadcast_maximum_fusion
  20.0 0.4 fusion.64
  20.4 5.6 %all-gather = bf16[128,128]{1,0:T(8,128)(2,1)} all-gather(bf16[32,128]{1,0:T(8,128)(2,1)S(1)} %copy-done.20), channel_id=2, replica_groups=mesh['slab'=8,'head'=4] {'head'}, dimensions={0}, use_global_device_ids=true | all-gather | bytes 40960 | tf_op jit(solution)/shard_map/all_gather | solution.py:114
  26.1 0.6 copy-done.17
  26.7 1.7 fusion.37
  28.4 1.2 reshape.129
  29.7 0.9 copy.25
  30.6 0.3 reshape.130
  30.9 0.9 copy.26
  31.8 0.3 reshape.132
  32.1 0.9 copy.28
  33.0 0.3 reshape.131
  33.5 2.0 pad_maximum_fusion.1
  35.5 0.3 fusion.5
  35.8 0.8 copy-done.6
  36.6 1.0 fusion.77
  37.6 3.8 %fusion.29 = f32[2,16,32,32]{3,2,1,0:T(8,128)} fusion(bf16[2,2,16,128,32]{3,4,2,1,0:T(8,128)(2,1)S(1)} %pad_maximum_fusion.1, f32[2,16,32]{2,1,0:T(8,128)S(1)} %get-tuple-element.33, f32[2,16,32,128]{3,2,1,0:T(8,128)} %copy-done.6), kind=kOutput, calls=%fused_computation.63 | convolution fusion | flops 8782975 | bytes 1458176 | tf_op jit(solution)/shard_map/sbqk,sbkd->sbqd/dot_general | solution.py:103
  41.5 1.9 copy.48
  43.4 1.3 copy.47
  44.6 1.0 multiply_convert_fusion.3
  45.6 5.8 %all_gather.6 = bf16[4,2,512,32]{2,3,0,1:T(8,128)(2,1)S(1)} all-gather(bf16[1,2,512,32]{2,3,0,1:T(8,128)(2,1)S(1)} %multiply_convert_fusion.3), channel_id=1, replica_groups=mesh['slab'=8,'head'=4] {'head'}, dimensions={0}, use_global_device_ids=true | all-gather | bytes 327680 | tf_op jit(solution)/shard_map/all_gather | solution.py:113
  51.4 0.5 convolution_convert_fusion
  52.1 0.3 fusion.51
  52.4 1.0 fusion.8
  53.4 0.5 fusion.3
  53.9 0.3 copy-done.12
  54.2 1.1 convolution_convert_fusion.1
  55.3 0.2 all-reduce.13.cloned.1.call-start
  55.5 0.9 convolution_bitcast_fusion.4
  56.4 34.3 %all-reduce.11.cloned.1.call-done = bf16[2,512,128]{2,1,0:T(8,128)(2,1)} async-done(((bf16[2,512,128]{2,1,0:T(8,128)(2,1)}), bf16[2,512,128]{2,1,0:T(8,128)(2,1)}) %all-reduce.11.cloned.1.call-update) | async-done | bytes 262160 | tf_op jit(solution)/shard_map/psum | solution.py:137
  90.7 1.9 fusion.42
  92.8 3.8 %convolution_bitcast_fusion.1 = f32[1,2,16,128,32]{3,4,2,1,0:T(8,128)} fusion(bf16[2,16,32,32]{2,1,3,0:T(8,128)(2,1)S(1)} %reshape.135, f32[2,16,32]{2,1,0:T(8,128)S(1)} %get-tuple-element.33, f32[2,16,32,128]{3,2,1,0:T(8,128)} %copy-done.6), kind=kOutput, calls=%fused_computation.14 | convolution fusion | flops 8782975 | bytes 1118208 | tf_op jit(solution)/shard_map/sbqk,sbqd->sbkd/dot_general | solution.py:165
  96.6 1.6 multiply_reduce_fusion
  98.3 0.3 fusion.71
  98.6 1.0 fusion.6
  99.6 0.2 convolution_bitcast_fusion.2
  99.8 1.0 convolution_bitcast_fusion.7
  100.8 2.2 fusion.10
  103.0 1.6 copy.35
  104.6 2.3 reshape.136
  106.9 2.8 %copy.36 = f32[2,2,16,32,32]{3,2,4,1,0:T(8,128)} copy(f32[2,2,16,32,32]{3,4,2,1,0:T(8,128)} %get-tuple-element.14) | data formatting | bytes 524288 | tf_op jit(solution)/shard_map/slice | solution.py:49
  109.7 2.3 reshape.137
  112.1 2.8 %copy.38 = f32[2,2,16,32,32]{3,2,4,1,0:T(8,128)} copy(f32[2,2,16,32,32]{3,4,2,1,0:T(8,128)} %get-tuple-element.15) | data formatting | bytes 524288 | tf_op jit(solution)/shard_map/slice | solution.py:49
  114.9 2.3 reshape.139
  117.2 1.6 copy.37
  118.8 1.7 reshape.138
  120.4 1.5 fusion.72
  122.0 3.4 %collective-permute-start.2 = (bf16[2,2,48,32]{2,3,1,0:T(8,128)(2,1)S(1)}, bf16[2,2,48,32]{2,3,1,0:T(8,128)(2,1)S(1)}, u32[]{:S(2)}, u32[]{:S(2)}) collective-permute-start(bf16[2,2,48,32]{2,3,1,0:T(8,128)(2,1)S(1)} %get-tuple-element.21), channel_id=1, source_target_pairs={{0,4},{4,8},{8,12},{12,16},{16,20},{20,24},{24,28},{1,5},{5,9},{9,... | collective-permute-start | bytes 36872 | tf_op jit(solution)/shard_map/ppermute | solution.py:20
  125.4 1.3 collective-permute-start.3
  126.7 1.2 convolution_bitcast_fusion.6
  127.9 38.2 %all-reduce.6 = (f32[32,128]{1,0:T(8,128)S(1)}, f32[16,1]{0,1:T(1,128)S(1)}) all-reduce(f32[32,128]{1,0:T(8,128)S(1)} %convolution_bitcast_fusion.6, f32[16,1]{0,1:T(1,128)S(1)} %convolution_bitcast_fusion.7), channel_id=1, replica_groups=mesh['slab'=8,'head'=4] {'slab'}, use_global_device_ids=true, to_apply=%region_9.10 | all-reduce | flops 4112 | bytes 32896 | tf_op jit(solution)/shard_map/psum | solution.py:195
  166.1 0.6 broadcast_multiply_fusion.2
  167.3 1.1 convolution_bitcast_fusion.5
  168.4 0.5 broadcast_multiply_fusion.4
  168.9 66.0 %all-reduce.13.cloned.1.call-done = (f32[4,128,32]{1,2,0:T(8,128)}, f32[128,192]{0,1:T(8,128)}) async-done(((f32[4,128,32]{1,2,0:T(8,128)}, f32[128,192]{0,1:T(8,128)}), (f32[4,128,32]{1,2,0:T(8,128)}, f32[128,192]{0,1:T(8,128)})) %all-reduce.13.cloned.1.call-update) | async-done | bytes 163856 | tf_op jit(solution)/shard_map/psum | solution.py:195
  234.9 1.5 broadcast_multiply_fusion.1
  236.4 1.5 broadcast_multiply_fusion
  (76 shorter events, 1.6 us)
Async XLA Ops:
  7.2 12.8 %copy-start = (bf16[512,16,128]{2,1,0:T(8,128)(2,1)S(1)}, bf16[512,16,128]{2,1,0:T(8,128)(2,1)}, u32[]{:S(2)}) copy-start(bf16[512,16,128]{2,1,0:T(8,128)(2,1)} %param.9) | copy-start | bytes 6291460
  7.2 12.8 %copy-start.22 = (bf16[16,1]{0,1:T(2,128)(2,1)S(1)}, bf16[16,1]{0,1:T(2,128)(2,1)}, u32[]{:S(2)}) copy-start(bf16[16,1]{0,1:T(2,128)(2,1)} %param.13) | copy-start | bytes 100
  7.2 83.5 %all-reduce.11.cloned.1.call-start = ((), (), s32[]{:S(2)}) async-start(), calls=%async_computation | async-start | bytes 524288 | tf_op jit(solution)/shard_map/psum | solution.py:137
  8.5 1.3 copy-start.15
  9.8 7.8 %copy-start.18 = (f32[2,512]{1,0:T(2,128)}, f32[2,512]{1,0:T(2,128)S(1)}, u32[]{:S(2)}) copy-start(f32[2,512]{1,0:T(2,128)S(1)} %add_rsqrt_fusion) | copy-start | bytes 12292
  9.8 10.6 %copy-start.20 = (bf16[32,128]{1,0:T(8,128)(2,1)S(1)}, bf16[32,128]{1,0:T(8,128)(2,1)}, u32[]{:S(2)}) copy-start(bf16[32,128]{1,0:T(8,128)(2,1)} %param.12) | copy-start | bytes 24580
  11.3 17.1 %copy-start.7 = (f32[4,2,512,32]{2,3,0,1:T(8,128)}, f32[4,2,512,32]{2,3,0,1:T(8,128)S(1)}, u32[]{:S(2)}) copy-start(f32[4,2,512,32]{2,3,0,1:T(8,128)S(1)} %get-tuple-element.32) | copy-start | bytes 1572868
  11.4 14.6 %collective-permute-start = (bf16[2,2,48,32]{2,3,0,1:T(8,128)(2,1)S(1)}, bf16[2,2,48,32]{2,3,0,1:T(8,128)(2,1)S(1)}, u32[]{:S(2)}, u32[]{:S(2)}) collective-permute-start(bf16[2,2,48,32]{2,3,0,1:T(8,128)(2,1)S(1)} %get-tuple-element.19), channel_id=1, source_target_pairs={{0,4},{4,8},{8,12},{12,16},{16,20},{20,24},{24,28},{1,5},{5,9},{9,... | collective-permute-start | bytes 36872 | tf_op jit(solution)/shard_map/ppermute | solution.py:20
  16.3 10.4 %collective-permute-start.1 = (bf16[2,2,48,32]{2,3,0,1:T(8,128)(2,1)S(1)}, bf16[2,2,48,32]{2,3,0,1:T(8,128)(2,1)}, u32[]{:S(2)}, u32[]{:S(2)}) collective-permute-start(bf16[2,2,48,32]{2,3,0,1:T(8,128)(2,1)S(1)} %get-tuple-element.20), channel_id=1, source_target_pairs={{4,0},{8,4},{12,8},{16,12},{20,16},{24,20},{28,24},{5,1},{9,5},{13... | collective-permute-start | bytes 36872 | tf_op jit(solution)/shard_map/ppermute | solution.py:22
  18.3 1.5 copy-start.23
  20.0 6.7 %copy-start.10 = (bf16[2,2,512,32]{2,3,0,1:T(8,128)(2,1)S(1)}, bf16[2,2,512,32]{2,3,0,1:T(8,128)(2,1)}, u32[]{:S(2)}) copy-start(bf16[2,2,512,32]{2,3,0,1:T(8,128)(2,1)} %slice.103) | copy-start | bytes 393220
  26.1 0.6 copy-start.17
  35.5 6.0 %copy-start.2 = (bf16[2,2,16,128,32]{3,4,2,1,0:T(8,128)(2,1)}, bf16[2,2,16,128,32]{3,4,2,1,0:T(8,128)(2,1)S(1)}, u32[]{:S(2)}) copy-start(bf16[2,2,16,128,32]{3,4,2,1,0:T(8,128)(2,1)S(1)} %pad_maximum_fusion.1) | copy-start | bytes 1572868
  35.8 0.8 copy-start.6
  37.6 13.8 %copy-start.14 = (bf16[128,128]{1,0:T(8,128)(2,1)S(1)}, bf16[128,128]{1,0:T(8,128)(2,1)}, u32[]{:S(2)}) copy-start(bf16[128,128]{1,0:T(8,128)(2,1)} %all-gather) | copy-start | bytes 98308
  43.4 8.8 %copy-start.1 = (bf16[2,512,128]{2,1,0:T(8,128)(2,1)S(1)}, bf16[2,512,128]{2,1,0:T(8,128)(2,1)}, u32[]{:S(2)}) copy-start(bf16[2,512,128]{2,1,0:T(8,128)(2,1)} %param.8) | copy-start | bytes 786436
  43.4 8.8 %copy-start.11 = (bf16[128,192]{0,1:T(8,128)(2,1)S(1)}, bf16[128,192]{0,1:T(8,128)(2,1)}, u32[]{:S(2)}) copy-start(bf16[128,192]{0,1:T(8,128)(2,1)} %param.14) | copy-start | bytes 147460
  51.4 1.0 copy-start.21
  51.4 1.0 copy-start.24
  51.4 1.0 copy-start.26
  52.4 1.0 copy-start.25
  53.4 0.8 copy-start.12
  55.3 179.6 %all-reduce.13.cloned.1.call-start = ((), (), s32[]{:S(2)}) async-start(), calls=%async_computation.1 | async-start | bytes 327680 | tf_op jit(solution)/shard_map/psum | solution.py:195
  56.4 40.2 %copy-start.3 = (bf16[2,2,16,128,32]{3,4,2,1,0:T(8,128)(2,1)S(1)}, bf16[2,2,16,128,32]{3,4,2,1,0:T(8,128)(2,1)}, u32[]{:S(2)}) copy-start(bf16[2,2,16,128,32]{3,4,2,1,0:T(8,128)(2,1)} %copy-done.2) | copy-start | bytes 1572868
  96.6 1.6 copy-start.5
  96.6 2.0 copy-start.4
  99.6 1.2 copy-start.9
  117.2 9.5 %copy-start.13 = (f32[2,512,32]{1,2,0:T(8,128)S(1)}, f32[2,512,32]{1,2,0:T(8,128)}, u32[]{:S(2)}) copy-start(f32[2,512,32]{1,2,0:T(8,128)} %copy.48) | copy-start | bytes 393220
  118.8 48.0 %copy-start.8 = (bf16[2,16,32,32]{3,2,1,0:T(8,128)(2,1)S(1)}, bf16[2,16,32,32]{3,2,1,0:T(8,128)(2,1)}, u32[]{:S(2)}) copy-start(bf16[2,16,32,32]{3,2,1,0:T(8,128)(2,1)} %fusion.6) | copy-start | bytes 196612
  120.4 46.8 %copy-start.16 = (f32[2,512]{1,0:T(2,128)S(1)}, f32[2,512]{1,0:T(2,128)}, u32[]{:S(2)}) copy-start(f32[2,512]{1,0:T(2,128)} %copy-done.15) | copy-start | bytes 12292
  120.4 46.8 %copy-start.19 = (f32[2,512]{1,0:T(2,128)S(1)}, f32[2,512]{1,0:T(2,128)}, u32[]{:S(2)}) copy-start(f32[2,512]{1,0:T(2,128)} %copy-done.18) | copy-start | bytes 12292
  120.4 46.8 %copy-start.27 = (bf16[1,2,512,32]{2,3,1,0:T(8,128)(2,1)S(1)}, bf16[1,2,512,32]{2,3,1,0:T(8,128)(2,1)}, u32[]{:S(2)}) copy-start(bf16[1,2,512,32]{2,3,1,0:T(8,128)(2,1)} %get-tuple-element.18) | copy-start | bytes 196612
  122.0 44.9 %collective-permute-start.2 = (bf16[2,2,48,32]{2,3,1,0:T(8,128)(2,1)S(1)}, bf16[2,2,48,32]{2,3,1,0:T(8,128)(2,1)S(1)}, u32[]{:S(2)}, u32[]{:S(2)}) collective-permute-start(bf16[2,2,48,32]{2,3,1,0:T(8,128)(2,1)S(1)} %get-tuple-element.21), channel_id=1, source_target_pairs={{0,4},{4,8},{8,12},{12,16},{16,20},{20,24},{24,28},{1,5},{5,9},{9,... | collective-permute-start | bytes 36872 | tf_op jit(solution)/shard_map/ppermute | solution.py:20
  125.4 41.5 %collective-permute-start.3 = (bf16[2,2,48,32]{2,3,1,0:T(8,128)(2,1)S(1)}, bf16[2,2,48,32]{2,3,1,0:T(8,128)(2,1)S(1)}, u32[]{:S(2)}, u32[]{:S(2)}) collective-permute-start(bf16[2,2,48,32]{2,3,1,0:T(8,128)(2,1)S(1)} %get-tuple-element.22), channel_id=1, source_target_pairs={{4,0},{8,4},{12,8},{16,12},{20,16},{24,20},{28,24},{5,1},{9,5},{13... | collective-permute-start | bytes 36872 | tf_op jit(solution)/shard_map/ppermute | solution.py:22
Sparse Core Ops, SparseCore 0:
  55.4 35.2 all-reduce.10
  168.5 66.3 all-reduce.12
where the time goes:
time: 246 us; the launch traced here: 245 us
  waiting for transfers between devices  100 us (41%)
  blocking collectives  49.7 us (20%)
  local copies, waits for them, and re-layouts  28.7 us (12%)
  matrix products  22 us (9%)
  other arithmetic  18.4 us (7%)
  between operations  14.5 us (6%)
  starting transfers between devices  11.1 us (5%)
    psum x1, waiting for transfers between devices, on_device(): lax.psum((grad_proj_local, grad_out_local, grad_pair_local, grad_tok_loca...  66 us
    psum x1, blocking collectives, on_device(): lax.psum((grad_proj_local, grad_out_local, grad_pair_local, grad_tok_loca...  38.2 us
    psum x1, waiting for transfers between devices, on_device(): mixed_grad = lax.psum(mixed_terms.astype(jnp.bfloat16), 'head')  34.3 us
    slice x4, local copies, waits for them, and re-layouts, key_unwindowed_rows(): windowed[..., Q_WIN * offset:Q_WIN * (offset + 1), :]  8.83 us
    reshape x4, local copies, waits for them, and re-layouts, key_unwindowed_rows(): windowed[..., Q_WIN * offset:Q_WIN * (offset + 1), :]  8.59 us
    ppermute x2, starting transfers between devices, extended_2(): lax.ppermute(tail, axis, [(i, (i + 1) % count) for i in range(ends)])  8.23 us
    all_gather x1, blocking collectives, on_device(): lax.all_gather(heads_out[None], 'head', axis=0, tiled=True)  5.85 us
    all_gather x1, blocking collectives, on_device(): lax.all_gather(w_out[None], 'head', axis=0, tiled=True)  5.64 us
  transfers between devices with their start and end apart: 6, of which 2 were waited for; matrix products, arithmetic and copies ran while one was open for 2% of the time, Pallas kernels for 0%

commit v1 on v0

--- a/solution.py
+++ b/solution.py
@@ -134,7 +134,12 @@
         "saw,sah->wh", mixed_half, act_grad, preferred_element_type=jnp.float32
     )
     mixed_terms = jnp.einsum("sah,wh->saw", act_grad, w_tok, preferred_element_type=jnp.float32)
-    mixed_grad = lax.psum(mixed_terms.astype(jnp.bfloat16), "head")
+
+    def move_series_all(target):
+        x_now = lax.all_gather(target, "head").sum(axis=0)
+        return x_now
+
+    mixed_grad = move_series_all(mixed_terms.astype(jnp.bfloat16))
     out_grad = jnp.einsum("saw,dw->sad", mixed_grad, w_out, preferred_element_type=jnp.float32)
     grad_out_local = jnp.einsum(
         "sad,saw->dw", heads_out, mixed_grad, preferred_element_type=jnp.float32

time: 246 us -> 230 us (0.935)
  waiting for transfers between devices: 100 us -> 80.8 us
    psum x1 -> x0, waiting for transfers between devices: 34.3 us -> none  [on_device(): mixed_grad = lax.psum(mixed_terms.astype(jnp.bfloat16), 'head')]
    all_gather x0 -> x1, waiting for transfers between devices: none -> 14.7 us  [move_series_all(): x_now = lax.all_gather(target, 'head').sum(axis=0)]
  transfers between devices with their start and end apart: 6 -> 6, of which waited for: 2 -> 2; matrix products, arithmetic and copies ran while one was open for 2% -> 4% of each run, Pallas kernels for 0% -> 0%
where the time goes in v1:
time: 230 us; the launch traced here: 229 us
  waiting for transfers between devices  80.8 us (35%)
  blocking collectives  49.8 us (22%)
  local copies, waits for them, and re-layouts  29.8 us (13%)
  matrix products  23.6 us (10%)
  other arithmetic  19.8 us (9%)
  between operations  14.5 us (6%)
  starting transfers between devices  11.1 us (5%)
    psum x1, waiting for transfers between devices, on_device(): lax.psum((grad_proj_local, grad_out_local, grad_pair_local, grad_tok_loca...  66.1 us
    psum x1, blocking collectives, on_device(): lax.psum((grad_proj_local, grad_out_local, grad_pair_local, grad_tok_loca...  38.3 us
    all_gather x1, waiting for transfers between devices, move_series_all(): x_now = lax.all_gather(target, 'head').sum(axis=0)  14.7 us
    slice x4, local copies, waits for them, and re-layouts, key_unwindowed_rows(): windowed[..., Q_WIN * offset:Q_WIN * (offset + 1), :]  8.8 us
    reshape x4, local copies, waits for them, and re-layouts, key_unwindowed_rows(): windowed[..., Q_WIN * offset:Q_WIN * (offset + 1), :]  8.62 us
    ppermute x2, starting transfers between devices, extended_2(): lax.ppermute(tail, axis, [(i, (i + 1) % count) for i in range(ends)])  8.24 us
    all_gather x1, blocking collectives, on_device(): lax.all_gather(heads_out[None], 'head', axis=0, tiled=True)  5.85 us
    all_gather x1, blocking collectives, on_device(): lax.all_gather(w_out[None], 'head', axis=0, tiled=True)  5.64 us
  transfers between devices with their start and end apart: 6, of which 2 were waited for; matrix products, arithmetic and copies ran while one was open for 4% of the time, Pallas kernels for 0%

profile of v1, /device:TPU:0, one launch (start us, length us, event | category | flops | bytes accessed | tf_op | source)
XLA Modules:
  0.0 229.4 jit_solution(14599161264125893007)
XLA Ops:
  7.2 1.2 convert_reduce_fusion.1
  8.5 1.3 fusion.14
  9.9 1.5 fusion.76
  11.4 4.9 %collective-permute-start = (bf16[2,2,48,32]{2,3,0,1:T(8,128)(2,1)S(1)}, bf16[2,2,48,32]{2,3,0,1:T(8,128)(2,1)S(1)}, u32[]{:S(2)}, u32[]{:S(2)}) collective-permute-start(bf16[2,2,48,32]{2,3,0,1:T(8,128)(2,1)S(1)} %get-tuple-element.19), channel_id=1, source_target_pairs={{0,4},{4,8},{8,12},{12,16},{16,20},{20,24},{24,28},{1,5},{5,9},{9,... | collective-permute-start | bytes 36872 | tf_op jit(solution)/shard_map/ppermute | solution.py:20
  16.3 1.3 collective-permute-start.1
  17.6 0.7 slice.103
  18.3 0.9 convert_reduce_fusion.2
  19.2 0.5 broadcast_maximum_fusion
  20.0 0.4 fusion.64
  20.4 5.6 %all-gather = bf16[128,128]{1,0:T(8,128)(2,1)} all-gather(bf16[32,128]{1,0:T(8,128)(2,1)S(1)} %copy-done.22), channel_id=2, replica_groups=mesh['slab'=8,'head'=4] {'head'}, dimensions={0}, use_global_device_ids=true | all-gather | bytes 40960 | tf_op jit(solution)/shard_map/all_gather | solution.py:114
  26.1 0.6 copy-done.18
  26.7 1.7 fusion.37
  28.4 1.2 reshape.129
  29.7 1.0 copy.41
  30.6 0.3 reshape.130
  30.9 0.9 copy.42
  31.9 0.3 reshape.132
  32.1 0.9 copy.44
  33.1 0.3 reshape.131
  33.5 2.0 pad_maximum_fusion.1
  35.6 0.3 fusion.5
  35.9 0.8 copy-done.6
  36.7 1.0 fusion.77
  37.7 3.8 %fusion.29 = f32[2,16,32,32]{3,2,1,0:T(8,128)} fusion(bf16[2,2,16,128,32]{3,4,2,1,0:T(8,128)(2,1)S(1)} %pad_maximum_fusion.1, f32[2,16,32]{2,1,0:T(8,128)S(1)} %get-tuple-element.33, f32[2,16,32,128]{3,2,1,0:T(8,128)} %copy-done.6), kind=kOutput, calls=%fused_computation.63 | convolution fusion | flops 8782975 | bytes 1458176 | tf_op jit(solution)/shard_map/sbqk,sbkd->sbqd/dot_general | solution.py:103
  41.5 1.3 copy.63
  42.8 1.0 multiply_convert_fusion.3
  43.7 5.9 %all_gather.12 = bf16[4,2,512,32]{2,3,0,1:T(8,128)(2,1)S(1)} all-gather(bf16[1,2,512,32]{2,3,0,1:T(8,128)(2,1)S(1)} %multiply_convert_fusion.3), channel_id=1, replica_groups=mesh['slab'=8,'head'=4] {'head'}, dimensions={0}, use_global_device_ids=true | all-gather | bytes 327680 | tf_op jit(solution)/shard_map/all_gather | solution.py:113
  49.6 0.5 convolution_convert_fusion
  50.3 0.3 fusion.51
  50.6 0.5 fusion.3
  51.1 0.4 copy-done.9
  51.6 1.1 convolution_convert_fusion.1
  52.9 1.9 copy.64
  54.7 0.9 convolution_bitcast_fusion.4
  55.6 2.1 fusion.8
  57.8 14.7 %all-gather.4.cloned.1.call-done = bf16[8,512,128]{2,1,0:T(8,128)(2,1)} async-done(((bf16[2,512,128]{2,1,0:T(8,128)(2,1)}), bf16[8,512,128]{2,1,0:T(8,128)(2,1)}) %all-gather.4.cloned.1.call-update) | async-done | bytes 1048592 | tf_op jit(solution)/shard_map/all_gather | solution.py:139
  72.5 1.5 reduce_sum.83
  74.0 1.7 convolution_bitcast_fusion.6
  75.7 1.8 fusion.42
  77.5 1.0 reshape.135
  78.5 3.8 %convolution_bitcast_fusion.1 = f32[1,2,16,128,32]{3,4,2,1,0:T(8,128)} fusion(bf16[2,16,32,32]{2,1,3,0:T(8,128)(2,1)S(1)} %reshape.135, f32[2,16,32]{2,1,0:T(8,128)S(1)} %get-tuple-element.33, f32[2,16,32,128]{3,2,1,0:T(8,128)} %copy-done.6), kind=kOutput, calls=%fused_computation.14 | convolution fusion | flops 8782975 | bytes 1118208 | tf_op jit(solution)/shard_map/sbqk,sbqd->sbkd/dot_general | solution.py:170
  82.4 1.6 multiply_reduce_fusion
  84.0 0.3 fusion.71
  84.3 1.0 fusion.6
  85.5 1.0 convolution_bitcast_fusion.7
  86.5 2.3 fusion.10
  88.7 1.6 copy.51
  90.3 2.3 %reshape.136 = f32[2,2,512,32]{2,3,1,0:T(8,128)} reshape(f32[2,2,16,32,32]{3,2,4,1,0:T(8,128)} %copy.51) | data formatting | bytes 524288 | tf_op jit(solution)/shard_map/reshape | solution.py:49
  92.6 2.8 %copy.52 = f32[2,2,16,32,32]{3,2,4,1,0:T(8,128)} copy(f32[2,2,16,32,32]{3,4,2,1,0:T(8,128)} %get-tuple-element.14) | data formatting | bytes 524288 | tf_op jit(solution)/shard_map/slice | solution.py:49
  95.4 2.3 %reshape.137 = f32[2,2,512,32]{2,3,1,0:T(8,128)} reshape(f32[2,2,16,32,32]{3,2,4,1,0:T(8,128)} %copy.52) | data formatting | bytes 524288 | tf_op jit(solution)/shard_map/reshape | solution.py:49
  97.8 2.8 %copy.54 = f32[2,2,16,32,32]{3,2,4,1,0:T(8,128)} copy(f32[2,2,16,32,32]{3,4,2,1,0:T(8,128)} %get-tuple-element.15) | data formatting | bytes 524288 | tf_op jit(solution)/shard_map/slice | solution.py:49
  100.6 2.3 %reshape.139 = f32[2,2,512,32]{2,3,1,0:T(8,128)} reshape(f32[2,2,16,32,32]{3,2,4,1,0:T(8,128)} %copy.54) | data formatting | bytes 524288 | tf_op jit(solution)/shard_map/reshape | solution.py:49
  102.9 1.6 copy.53
  104.5 1.7 reshape.138
  106.2 1.4 fusion.72
  107.7 3.4 %collective-permute-start.2 = (bf16[2,2,48,32]{2,3,1,0:T(8,128)(2,1)S(1)}, bf16[2,2,48,32]{2,3,1,0:T(8,128)(2,1)S(1)}, u32[]{:S(2)}, u32[]{:S(2)}) collective-permute-start(bf16[2,2,48,32]{2,3,1,0:T(8,128)(2,1)S(1)} %get-tuple-element.21), channel_id=1, source_target_pairs={{0,4},{4,8},{8,12},{12,16},{16,20},{20,24},{24,28},{1,5},{5,9},{9,... | collective-permute-start | bytes 36872 | tf_op jit(solution)/shard_map/ppermute | solution.py:20
  111.1 1.3 collective-permute-start.3
  112.4 38.3 %all-reduce.6 = (f32[32,128]{1,0:T(8,128)S(1)}, f32[16,1]{0,1:T(1,128)S(1)}) all-reduce(f32[32,128]{1,0:T(8,128)S(1)} %copy-done.21, f32[16,1]{0,1:T(1,128)S(1)} %convolution_bitcast_fusion.7), channel_id=1, replica_groups=mesh['slab'=8,'head'=4] {'slab'}, use_global_device_ids=true, to_apply=%region_9.10 | all-reduce | flops 4112 | bytes 32896 | tf_op jit(solution)/shard_map/psum | solution.py:200
  150.7 0.6 broadcast_multiply_fusion.2
  151.8 1.1 convolution_bitcast_fusion.5
  153.0 0.5 broadcast_multiply_fusion.4
  153.5 66.1 %all-reduce.10.cloned.1.call-done = (f32[4,128,32]{1,2,0:T(8,128)}, f32[128,192]{0,1:T(8,128)}) async-done(((f32[4,128,32]{1,2,0:T(8,128)}, f32[128,192]{0,1:T(8,128)}), (f32[4,128,32]{1,2,0:T(8,128)}, f32[128,192]{0,1:T(8,128)})) %all-reduce.10.cloned.1.call-update) | async-done | bytes 163856 | tf_op jit(solution)/shard_map/psum | solution.py:200
  219.6 1.5 broadcast_multiply_fusion.1
  221.0 1.5 broadcast_multiply_fusion
  (81 shorter events, 1.8 us)
Async XLA Ops:
  7.2 12.8 %copy-start = (bf16[512,16,128]{2,1,0:T(8,128)(2,1)S(1)}, bf16[512,16,128]{2,1,0:T(8,128)(2,1)}, u32[]{:S(2)}) copy-start(bf16[512,16,128]{2,1,0:T(8,128)(2,1)} %param.9) | copy-start | bytes 6291460
  7.2 12.8 %copy-start.24 = (bf16[16,1]{0,1:T(2,128)(2,1)S(1)}, bf16[16,1]{0,1:T(2,128)(2,1)}, u32[]{:S(2)}) copy-start(bf16[16,1]{0,1:T(2,128)(2,1)} %param.13) | copy-start | bytes 100
  7.2 65.3 %all-gather.4.cloned.1.call-start = ((), (), s32[]{:S(2)}) async-start(), calls=%async_computation | async-start | bytes 1310720 | tf_op jit(solution)/shard_map/all_gather | solution.py:139
  8.5 1.3 copy-start.16
  9.8 7.8 %copy-start.19 = (f32[2,512]{1,0:T(2,128)}, f32[2,512]{1,0:T(2,128)S(1)}, u32[]{:S(2)}) copy-start(f32[2,512]{1,0:T(2,128)S(1)} %add_rsqrt_fusion) | copy-start | bytes 12292
  9.8 10.6 %copy-start.22 = (bf16[32,128]{1,0:T(8,128)(2,1)S(1)}, bf16[32,128]{1,0:T(8,128)(2,1)}, u32[]{:S(2)}) copy-start(bf16[32,128]{1,0:T(8,128)(2,1)} %param.12) | copy-start | bytes 24580
  11.3 17.1 %copy-start.7 = (f32[4,2,512,32]{2,3,0,1:T(8,128)}, f32[4,2,512,32]{2,3,0,1:T(8,128)S(1)}, u32[]{:S(2)}) copy-start(f32[4,2,512,32]{2,3,0,1:T(8,128)S(1)} %get-tuple-element.32) | copy-start | bytes 1572868
  11.4 14.7 %collective-permute-start = (bf16[2,2,48,32]{2,3,0,1:T(8,128)(2,1)S(1)}, bf16[2,2,48,32]{2,3,0,1:T(8,128)(2,1)S(1)}, u32[]{:S(2)}, u32[]{:S(2)}) collective-permute-start(bf16[2,2,48,32]{2,3,0,1:T(8,128)(2,1)S(1)} %get-tuple-element.19), channel_id=1, source_target_pairs={{0,4},{4,8},{8,12},{12,16},{16,20},{20,24},{24,28},{1,5},{5,9},{9,... | collective-permute-start | bytes 36872 | tf_op jit(solution)/shard_map/ppermute | solution.py:20
  16.3 10.4 %collective-permute-start.1 = (bf16[2,2,48,32]{2,3,0,1:T(8,128)(2,1)S(1)}, bf16[2,2,48,32]{2,3,0,1:T(8,128)(2,1)}, u32[]{:S(2)}, u32[]{:S(2)}) collective-permute-start(bf16[2,2,48,32]{2,3,0,1:T(8,128)(2,1)S(1)} %get-tuple-element.20), channel_id=1, source_target_pairs={{4,0},{8,4},{12,8},{16,12},{20,16},{24,20},{28,24},{5,1},{9,5},{13... | collective-permute-start | bytes 36872 | tf_op jit(solution)/shard_map/ppermute | solution.py:22
  18.3 1.5 copy-start.25
  20.0 6.7 %copy-start.11 = (bf16[2,2,512,32]{2,3,0,1:T(8,128)(2,1)S(1)}, bf16[2,2,512,32]{2,3,0,1:T(8,128)(2,1)}, u32[]{:S(2)}) copy-start(bf16[2,2,512,32]{2,3,0,1:T(8,128)(2,1)} %slice.103) | copy-start | bytes 393220
  26.1 0.6 copy-start.18
  35.5 6.0 %copy-start.2 = (bf16[2,2,16,128,32]{3,4,2,1,0:T(8,128)(2,1)}, bf16[2,2,16,128,32]{3,4,2,1,0:T(8,128)(2,1)S(1)}, u32[]{:S(2)}) copy-start(bf16[2,2,16,128,32]{3,4,2,1,0:T(8,128)(2,1)S(1)} %pad_maximum_fusion.1) | copy-start | bytes 1572868
  35.8 0.8 copy-start.6
  37.7 11.9 %copy-start.15 = (bf16[128,128]{1,0:T(8,128)(2,1)S(1)}, bf16[128,128]{1,0:T(8,128)(2,1)}, u32[]{:S(2)}) copy-start(bf16[128,128]{1,0:T(8,128)(2,1)} %all-gather) | copy-start | bytes 98308
  41.5 8.8 %copy-start.1 = (bf16[2,512,128]{2,1,0:T(8,128)(2,1)S(1)}, bf16[2,512,128]{2,1,0:T(8,128)(2,1)}, u32[]{:S(2)}) copy-start(bf16[2,512,128]{2,1,0:T(8,128)(2,1)} %param.8) | copy-start | bytes 786436
  41.5 8.8 %copy-start.12 = (bf16[128,192]{0,1:T(8,128)(2,1)S(1)}, bf16[128,192]{0,1:T(8,128)(2,1)}, u32[]{:S(2)}) copy-start(bf16[128,192]{0,1:T(8,128)(2,1)} %param.14) | copy-start | bytes 147460
  49.6 1.0 copy-start.23
  49.6 1.0 copy-start.26
  49.6 1.0 copy-start.27
  49.6 1.0 copy-start.28
  50.6 0.9 copy-start.9
  50.6 0.9 copy-start.13
  52.6 166.9 %all-reduce.10.cloned.1.call-start = ((), (), s32[]{:S(2)}) async-start(), calls=%async_computation.1 | async-start | bytes 327680 | tf_op jit(solution)/shard_map/psum | solution.py:200
  55.6 18.3 %copy-start.14 = (f32[2,512,32]{1,2,0:T(8,128)S(1)}, f32[2,512,32]{1,2,0:T(8,128)}, u32[]{:S(2)}) copy-start(f32[2,512,32]{1,2,0:T(8,128)} %copy.64) | copy-start | bytes 393220
  74.0 8.4 %copy-start.3 = (bf16[2,2,16,128,32]{3,4,2,1,0:T(8,128)(2,1)S(1)}, bf16[2,2,16,128,32]{3,4,2,1,0:T(8,128)(2,1)}, u32[]{:S(2)}) copy-start(bf16[2,2,16,128,32]{3,4,2,1,0:T(8,128)(2,1)} %copy-done.2) | copy-start | bytes 1572868
  82.4 1.6 copy-start.5
  82.4 2.0 copy-start.4
  85.3 1.2 copy-start.10
  102.9 9.5 %copy-start.21 = (f32[32,128]{1,0:T(8,128)S(1)}, f32[32,128]{1,0:T(8,128)}, u32[]{:S(2)}) copy-start(f32[32,128]{1,0:T(8,128)} %convolution_bitcast_fusion.6) | copy-start | bytes 49156
  104.5 46.8 %copy-start.8 = (bf16[2,16,32,32]{3,2,1,0:T(8,128)(2,1)S(1)}, bf16[2,16,32,32]{3,2,1,0:T(8,128)(2,1)}, u32[]{:S(2)}) copy-start(bf16[2,16,32,32]{3,2,1,0:T(8,128)(2,1)} %fusion.6) | copy-start | bytes 196612
  104.5 47.3 %copy-start.17 = (f32[2,512]{1,0:T(2,128)S(1)}, f32[2,512]{1,0:T(2,128)}, u32[]{:S(2)}) copy-start(f32[2,512]{1,0:T(2,128)} %copy-done.16) | copy-start | bytes 12292
  104.5 47.3 %copy-start.20 = (f32[2,512]{1,0:T(2,128)S(1)}, f32[2,512]{1,0:T(2,128)}, u32[]{:S(2)}) copy-start(f32[2,512]{1,0:T(2,128)} %copy-done.19) | copy-start | bytes 12292
  104.5 47.3 %copy-start.29 = (bf16[1,2,512,32]{2,3,1,0:T(8,128)(2,1)S(1)}, bf16[1,2,512,32]{2,3,1,0:T(8,128)(2,1)}, u32[]{:S(2)}) copy-start(bf16[1,2,512,32]{2,3,1,0:T(8,128)(2,1)} %get-tuple-element.18) | copy-start | bytes 196612
  107.7 43.7 %collective-permute-start.2 = (bf16[2,2,48,32]{2,3,1,0:T(8,128)(2,1)S(1)}, bf16[2,2,48,32]{2,3,1,0:T(8,128)(2,1)S(1)}, u32[]{:S(2)}, u32[]{:S(2)}) collective-permute-start(bf16[2,2,48,32]{2,3,1,0:T(8,128)(2,1)S(1)} %get-tuple-element.21), channel_id=1, source_target_pairs={{0,4},{4,8},{8,12},{12,16},{16,20},{20,24},{24,28},{1,5},{5,9},{9,... | collective-permute-start | bytes 36872 | tf_op jit(solution)/shard_map/ppermute | solution.py:20
  111.1 40.3 %collective-permute-start.3 = (bf16[2,2,48,32]{2,3,1,0:T(8,128)(2,1)S(1)}, bf16[2,2,48,32]{2,3,1,0:T(8,128)(2,1)S(1)}, u32[]{:S(2)}, u32[]{:S(2)}) collective-permute-start(bf16[2,2,48,32]{2,3,1,0:T(8,128)(2,1)S(1)} %get-tuple-element.22), channel_id=1, source_target_pairs={{4,0},{8,4},{12,8},{16,12},{20,16},{24,20},{28,24},{5,1},{9,5},{13... | collective-permute-start | bytes 36872 | tf_op jit(solution)/shard_map/ppermute | solution.py:22
Sparse Core Ops, SparseCore 0:
  52.8 19.6 all-gather.3
  153.1 66.4 all-reduce.9
